TPU v7x, 32 devices: a whole 2x2x4 slice. The times are simulated.
32 devices in a mesh: fsdp: 4 (over z), tp: 4 (over y, core), sect: 2 (over x).
Axes of the slice: x: 2, y: 2, z: 4, core: 2. Of those that a mesh axis runs over, the one named last changes fastest.
Arguments:
- hidden: bfloat16 [4096, 8192], P('fsdp', 'sect'), may hold values from -6 to 6
- kv_weight: bfloat16 [8192, 2048], P(('sect', 'fsdp'), 'tp'), may hold values from -0.0625 to 0.0625
- readout: float32 [2048], P(('tp', 'sect')), may hold values from -0.125 to 0.125
- lengths: int32 [4, 4], P('fsdp'), may hold values from 1 to 512, as said below
- prompt_mask: int32 [4096], P('fsdp'), may hold values from 0 to 1, as said below
- group_ids: int32 [16], P('fsdp'), may hold values from 0 to 1
Outputs:
- keys_values: bfloat16 [4096, 2048], P('fsdp', ('tp', 'sect'))
- advantages: float32 [16], P('fsdp')
Inputs may be any that keep to these rules, and one draw needn't show every extreme that they name: `lengths`: each row sums to 1024; some entry of each row equals 512. `prompt_mask`: within each sequence the zeros come before the ones; at each index of fsdp exactly one sequence has no ones.
All inputs are finite; a program needn't handle non-finite values.
Results may differ from a plain program's by a relative error of at most 0.00045.
Values may be sent and summed in bfloat16 or wider, within the bound.
A program may use at most 64 MiB of HBM per device.

v0:
```python
import jax
import jax.numpy as jnp
from jax import lax
from jax.sharding import PartitionSpec as P


def swapped(value, axis, bit):
    mask = 2**bit
    pairs = [(source, source ^ mask) for source in range(lax.axis_size(axis))]
    return lax.ppermute(value, axis, pairs)


def local(hidden, kv_weight, readout, lengths, prompt_mask, group_ids):
    block_width = kv_weight.shape[1]
    col_width = block_width // lax.axis_size("sect")
    sect_index = lax.axis_index("sect")
    tok_rows = hidden.shape[0]

    def add_rows(piece):
        return jnp.dot(hidden, piece, preferred_element_type=jnp.float32)

    partner_cols = lax.dynamic_slice_in_dim(kv_weight, (1 - sect_index) * col_width, col_width, 1)
    partner_part = add_rows(lax.all_gather(partner_cols, "fsdp", axis=0, tiled=True))
    received = swapped(partner_part, "sect", 0)
    own_cols = lax.dynamic_slice_in_dim(kv_weight, sect_index * col_width, col_width, 1)
    own_part = add_rows(lax.all_gather(own_cols, "fsdp", axis=0, tiled=True))
    projected = own_part + received
    keys_values = projected.astype(jnp.bfloat16)
    partial_score = jnp.dot(projected, readout, precision=lax.Precision.HIGHEST)
    token_score = lax.psum(partial_score, ("tp", "sect"))
    mask_float = prompt_mask.astype(jnp.float32)
    row_len = lengths[0]
    finish = jnp.cumsum(row_len)
    starts = finish - row_len
    places = jnp.arange(tok_rows, dtype=jnp.int32)
    member = ((places[None, :] >= starts[:, None]) & (places[None, :] < finish[:, None])).astype(
        jnp.float32
    )
    seq_sum = jnp.dot(member, token_score * mask_float, precision=lax.Precision.HIGHEST)
    count = jnp.dot(member, mask_float, precision=lax.Precision.HIGHEST)
    reward = seq_sum / jnp.sqrt(jnp.maximum(count, 1.0))
    group_count = group_ids.shape[0] * lax.axis_size("fsdp") // 8
    onehot = (group_ids[:, None] == jnp.arange(group_count, dtype=jnp.int32)[None, :]).astype(
        jnp.float32
    )
    local_sizes = jnp.sum(onehot, axis=0)
    local_sums = jnp.sum(onehot * reward[:, None], axis=0)
    group_sums, group_sizes = lax.psum((local_sums, local_sizes), "fsdp")
    mean_g = group_sums / jnp.maximum(group_sizes, 1.0)
    own_mean = jnp.sum(onehot * mean_g[None, :], axis=1)
    local_dev = jnp.sum(onehot * ((reward - own_mean) ** 2)[:, None], axis=0)
    spread = lax.psum(local_dev, "fsdp")
    var_g = spread / jnp.maximum(group_sizes, 1.0)
    own_var = jnp.sum(onehot * var_g[None, :], axis=1)
    advantages = (reward - own_mean) / jnp.sqrt(own_var + 1.0)
    return (keys_values, advantages)


def solution(mesh):
    return jax.shard_map(
        local,
        mesh=mesh,
        in_specs=(
            P("fsdp", "sect"),
            P(("sect", "fsdp"), "tp"),
            P(("tp", "sect")),
            P("fsdp", None),
            P("fsdp"),
            P("fsdp"),
        ),
        out_specs=(P("fsdp", ("tp", "sect")), P("fsdp")),
        check_vma=False,
    )
```

profile of v0, /device:TPU:0, one launch (start us, length us, event | category | flops | bytes accessed | tf_op | source)
XLA Modules:
  0.0 153.3 jit_solution(12628619160099686405)
XLA Ops:
  7.2 0.0 copy-start
  7.2 0.0 all-gather.5.cloned.1.call-start
  7.2 2.2 %constant_dynamic-slice_fusion.1 = (bf16[1024,256]{1,0:T(8,128)(2,1)}, bf16[1024,256]{1,0:T(8,128)(2,1)}) fusion(bf16[1024,512]{1,0:T(8,128)(2,1)} %param.7, s32[]{:T(128)S(6)} %select_n.6, s32[]{:T(128)S(6)} %select_n.7), kind=kLoop, calls=%fused_computation.20 | loop fusion | bytes 2097160 | tf_op jit(solution)/shard_map/dynamic_slice | solution.py:25
  9.5 0.0 all-gather.5.cloned.1.call-update
  9.5 0.0 all-gather.3.cloned.1.call-start
  9.5 0.7 all-gather.3.cloned.1.call-update
  10.2 0.0 copy-start.3
  10.3 0.0 copy-start.1
  10.3 47.8 %all-gather.5.cloned.1.call-done = bf16[4096,256]{1,0:T(8,128)(2,1)} async-done(((bf16[1024,256]{1,0:T(8,128)(2,1)}), bf16[4096,256]{1,0:T(8,128)(2,1)}) %all-gather.5.cloned.1.call-update) | async-done | bytes 2097168 | tf_op jit(solution)/shard_map/all_gather | solution.py:23
  58.0 6.4 %convolution_bitcast_fusion = f32[1024,256]{0,1:T(8,128)S(1)} fusion(bf16[4096,256]{1,0:T(8,128)(2,1)} %all-gather.5.cloned.1.call-done, bf16[1024,4096]{1,0:T(8,128)(2,1)} %param.6), kind=kOutput, calls=%fused_computation | convolution fusion | flops 2147483648 | bytes 11534336 | tf_op jit(solution)/shard_map/dot_general | solution.py:20
  64.4 1.5 collective-permute-start
  66.0 0.0 copy-done.3
  66.0 0.2 reduce-window.7
  66.1 0.0 copy-done.1
  66.2 0.0 copy-start.2
  66.2 38.5 %all-gather.3.cloned.1.call-done = bf16[4096,256]{1,0:T(8,128)(2,1)} async-done(((bf16[1024,256]{1,0:T(8,128)(2,1)}), bf16[4096,256]{1,0:T(8,128)(2,1)}) %all-gather.3.cloned.1.call-update) | async-done | bytes 2097168 | tf_op jit(solution)/shard_map/all_gather | solution.py:26
  104.7 0.0 collective-permute-done
  104.7 6.4 %fusion.8 = (bf16[1024,256]{0,1:T(8,128)(2,1)S(1)}, f32[1024,256]{0,1:T(8,128)S(1)}) fusion(f32[1024,256]{0,1:T(8,128)S(1)} %collective-permute-done, bf16[4096,256]{1,0:T(8,128)(2,1)} %all-gather.3.cloned.1.call-done, bf16[1024,4096]{1,0:T(8,128)(2,1)} %param.6), kind=kOutput, calls=%fused_computation.25 | convolution fusion | flops 2148007936 | bytes 13107200 | tf_op jit(solution)/shard_map/dot_general | solution.py:20
  111.1 0.0 copy-done
  111.1 0.6 fusion.9
  111.8 13.5 %psum.28 = f32[1024]{0:T(1024)S(1)} all-reduce(f32[1024]{0:T(1024)S(1)} %bitcast.34), channel_id=1, replica_groups=mesh['fsdp'=4,'tp'=4,'sect'=2] {'tp','sect'}, use_global_device_ids=true, to_apply=%region_1.0 | all-reduce | flops 1024 | bytes 8192 | tf_op jit(solution)/shard_map/psum | solution.py:30
  125.3 0.2 convolution_bitcast_fusion.3
  125.5 0.2 fusion.3
  125.7 0.0 copy-done.2
  125.7 0.2 convert_reduce_fusion
  125.9 9.8 %all-reduce = (f32[2]{0:T(128)S(1)}, f32[2]{0:T(128)S(1)}) all-reduce(f32[2]{0:T(128)S(1)} %get-tuple-element.7, f32[2]{0:T(128)S(1)} %get-tuple-element.6), channel_id=1, replica_groups=mesh['fsdp'=4,'tp'=4,'sect'=2] {'fsdp'}, use_global_device_ids=true, to_apply=%region_3.4 | all-reduce | flops 4 | bytes 32 | tf_op jit(solution)/shard_map/psum | solution.py:48
  135.7 0.1 select_reduce_fusion.2
  135.8 0.1 select_reduce_fusion.1
  135.9 8.9 %psum.31 = f32[2]{0:T(128)S(1)} all-reduce(f32[2]{0:T(128)S(1)} %select_reduce_fusion.1), channel_id=1, replica_groups=mesh['fsdp'=4,'tp'=4,'sect'=2] {'fsdp'}, use_global_device_ids=true, to_apply=%region_8.9 | all-reduce | flops 2 | bytes 16 | tf_op jit(solution)/shard_map/psum | solution.py:52
  144.9 0.1 select_reduce_fusion
  145.0 1.0 copy.9
  146.0 0.5 rsqrt_multiply_fusion
  (6 shorter events, 0.0 us)
Async XLA Ops:
  7.2 104.0 %copy-start = (f32[256]{0:T(256)S(1)}, f32[256]{0:T(256)}, u32[]{:S(2)}) copy-start(f32[256]{0:T(256)} %param.8) | copy-start | bytes 3076
  7.2 50.9 %all-gather.5.cloned.1.call-start = ((), (), s32[]{:S(2)}) async-start(), calls=%async_computation.1 | async-start | bytes 2621440 | tf_op jit(solution)/shard_map/all_gather | solution.py:23
  9.5 95.2 %all-gather.3.cloned.1.call-start = ((), (), s32[]{:S(2)}) async-start(), calls=%async_computation | async-start | bytes 2621440 | tf_op jit(solution)/shard_map/all_gather | solution.py:26
  10.2 55.7 %copy-start.3 = (s32[1,4]{1,0:T(1,128)S(1)}, s32[1,4]{1,0:T(1,128)}, u32[]{:S(2)}) copy-start(s32[1,4]{1,0:T(1,128)} %param.9) | copy-start | bytes 52
  10.3 55.9 %copy-start.1 = (s32[1024]{0:T(1024)S(1)}, s32[1024]{0:T(1024)}, u32[]{:S(2)}) copy-start(s32[1024]{0:T(1024)} %param.10) | copy-start | bytes 12292
  64.4 40.3 %collective-permute-start = (f32[1024,256]{0,1:T(8,128)S(1)}, f32[1024,256]{0,1:T(8,128)S(1)}, u32[]{:S(2)}, u32[]{:S(2)}) collective-permute-start(f32[1024,256]{0,1:T(8,128)S(1)} %convolution_bitcast_fusion), channel_id=1, source_target_pairs={{0,1},{1,0},{2,3},{3,2},{4,5},{5,4},{6,7},{7,6},{8,9},{9,8},{10,11... | collective-permute-start | bytes 3145736 | tf_op jit(solution)/shard_map/ppermute | solution.py:10
  66.2 59.6 %copy-start.2 = (s32[4]{0:T(128)S(1)}, s32[4]{0:T(128)}, u32[]{:S(2)}) copy-start(s32[4]{0:T(128)} %param.11) | copy-start | bytes 52
Sparse Core Ops, SparseCore 0:
  9.6 48.3 all-gather.4
  60.2 44.4 all-gather.2
where the time goes:
time: 154 us; the launch traced here: 153 us
  waiting for transfers between devices  87 us (56%)
  blocking collectives  32.3 us (21%)
  between operations  14.1 us (9%)
  matrix products  13.9 us (9%)
  local copies, waits for them, and re-layouts  3.28 us (2%)
  starting transfers between devices  1.61 us (1%)
    all_gather x1, waiting for transfers between devices, local(): lax.all_gather(partner_cols, 'fsdp', axis=0, tiled=True)  47.8 us
    all_gather x1, waiting for transfers between devices, local(): own_part = add_rows(lax.all_gather(own_cols, 'fsdp', axis=0, tiled=True))  38.5 us
    psum x1, blocking collectives, local(): token_score = lax.psum(partial_score, ('tp', 'sect'))  13.5 us
    dot_general x2, matrix products, add_rows(): return jnp.dot(hidden, piece, preferred_element_type=jnp.float32)  12.8 us
    psum x1, blocking collectives, local(): group_sums, group_sizes = lax.psum((local_sums, local_sizes), 'fsdp')  9.81 us
    psum x1, blocking collectives, local(): spread = lax.psum(local_dev, 'fsdp')  8.94 us
  transfers between devices with their start and end apart: 3, of which 2 were waited for; matrix products, arithmetic and copies ran while one was open for 4% of the time, Pallas kernels for 0%

commit v1 on v0

--- a/solution.py
+++ b/solution.py
@@ -2,6 +2,7 @@
 import jax.numpy as jnp
 from jax import lax
 from jax.sharding import PartitionSpec as P
+from jax.lax import psum
 
 
 def swapped(value, axis, bit):
@@ -27,7 +28,9 @@
     projected = own_part + received
     keys_values = projected.astype(jnp.bfloat16)
     partial_score = jnp.dot(projected, readout, precision=lax.Precision.HIGHEST)
-    token_score = lax.psum(partial_score, ("tp", "sect"))
+    token_score = partial_score
+    for dev in ("sect", "tp"):
+        token_score = psum(token_score, dev)
     mask_float = prompt_mask.astype(jnp.float32)
     row_len = lengths[0]
     finish = jnp.cumsum(row_len)

time: 154 us -> 151 us (0.981)
  blocking collectives: 32.3 us -> 29.3 us
    psum x1 -> x2, blocking collectives: 13.5 us -> 10.6 us  [local(): token_score = psum(token_score, dev)]
where the time goes in v1:
time: 151 us; the launch traced here: 150 us
  waiting for transfers between devices  87 us (58%)
  blocking collectives  29.3 us (19%)
  between operations  14.1 us (9%)
  matrix products  13.9 us (9%)
  local copies, waits for them, and re-layouts  3.28 us (2%)
  starting transfers between devices  1.61 us (1%)
    all_gather x1, waiting for transfers between devices, local(): lax.all_gather(partner_cols, 'fsdp', axis=0, tiled=True)  47.8 us
    all_gather x1, waiting for transfers between devices, local(): own_part = add_rows(lax.all_gather(own_cols, 'fsdp', axis=0, tiled=True))  38.5 us
    dot_general x2, matrix products, add_rows(): return jnp.dot(hidden, piece, preferred_element_type=jnp.float32)  12.8 us
    psum x2, blocking collectives, local(): token_score = psum(token_score, dev)  10.6 us
    psum x1, blocking collectives, local(): group_sums, group_sizes = lax.psum((local_sums, local_sizes), 'fsdp')  9.75 us
    psum x1, blocking collectives, local(): spread = lax.psum(local_dev, 'fsdp')  9 us
  transfers between devices with their start and end apart: 3, of which 2 were waited for; matrix products, arithmetic and copies ran while one was open for 4% of the time, Pallas kernels for 0%

profile of v1, /device:TPU:0, one launch (start us, length us, event | category | flops | bytes accessed | tf_op | source)
XLA Modules:
  0.0 150.4 jit_solution(6823630262091178777)
XLA Ops:
  7.2 0.0 copy-start
  7.2 0.0 all-gather.5.cloned.1.call-start
  7.2 2.2 %constant_dynamic-slice_fusion.1 = (bf16[1024,256]{1,0:T(8,128)(2,1)}, bf16[1024,256]{1,0:T(8,128)(2,1)}) fusion(bf16[1024,512]{1,0:T(8,128)(2,1)} %param.7, s32[]{:T(128)S(6)} %select_n.6, s32[]{:T(128)S(6)} %select_n.7), kind=kLoop, calls=%fused_computation.20 | loop fusion | bytes 2097160 | tf_op jit(solution)/shard_map/dynamic_slice | solution.py:26
  9.5 0.0 all-gather.5.cloned.1.call-update
  9.5 0.0 all-gather.3.cloned.1.call-start
  9.5 0.7 all-gather.3.cloned.1.call-update
  10.2 0.0 copy-start.3
  10.3 0.0 copy-start.1
  10.3 47.8 %all-gather.5.cloned.1.call-done = bf16[4096,256]{1,0:T(8,128)(2,1)} async-done(((bf16[1024,256]{1,0:T(8,128)(2,1)}), bf16[4096,256]{1,0:T(8,128)(2,1)}) %all-gather.5.cloned.1.call-update) | async-done | bytes 2097168 | tf_op jit(solution)/shard_map/all_gather | solution.py:24
  58.0 6.4 %convolution_bitcast_fusion = f32[1024,256]{0,1:T(8,128)S(1)} fusion(bf16[4096,256]{1,0:T(8,128)(2,1)} %all-gather.5.cloned.1.call-done, bf16[1024,4096]{1,0:T(8,128)(2,1)} %param.6), kind=kOutput, calls=%fused_computation | convolution fusion | flops 2147483648 | bytes 11534336 | tf_op jit(solution)/shard_map/dot_general | solution.py:21
  64.4 1.5 %collective-permute-start = (f32[1024,256]{0,1:T(8,128)S(1)}, f32[1024,256]{0,1:T(8,128)S(1)}, u32[]{:S(2)}, u32[]{:S(2)}) collective-permute-start(f32[1024,256]{0,1:T(8,128)S(1)} %convolution_bitcast_fusion), channel_id=1, source_target_pairs={{0,1},{1,0},{2,3},{3,2},{4,5},{5,4},{6,7},{7,6},{8,9},{9,8},{10,11... | collective-permute-start | bytes 3145736 | tf_op jit(solution)/shard_map/ppermute | solution.py:11
  66.0 0.0 copy-done.3
  66.0 0.2 reduce-window.7
  66.1 0.0 copy-done.1
  66.2 0.0 copy-start.2
  66.2 38.5 %all-gather.3.cloned.1.call-done = bf16[4096,256]{1,0:T(8,128)(2,1)} async-done(((bf16[1024,256]{1,0:T(8,128)(2,1)}), bf16[4096,256]{1,0:T(8,128)(2,1)}) %all-gather.3.cloned.1.call-update) | async-done | bytes 2097168 | tf_op jit(solution)/shard_map/all_gather | solution.py:27
  104.7 0.0 collective-permute-done
  104.7 6.4 %fusion.8 = (bf16[1024,256]{0,1:T(8,128)(2,1)S(1)}, f32[1024,256]{0,1:T(8,128)S(1)}) fusion(f32[1024,256]{0,1:T(8,128)S(1)} %collective-permute-done, bf16[4096,256]{1,0:T(8,128)(2,1)} %all-gather.3.cloned.1.call-done, bf16[1024,4096]{1,0:T(8,128)(2,1)} %param.6), kind=kOutput, calls=%fused_computation.25 | convolution fusion | flops 2148007936 | bytes 13107200 | tf_op jit(solution)/shard_map/dot_general | solution.py:21
  111.1 0.0 copy-done
  111.1 0.6 fusion.9
  111.8 4.9 %psum.35 = f32[1024]{0:T(1024)S(1)} all-reduce(f32[1024]{0:T(1024)S(1)} %bitcast.34), channel_id=1, replica_groups=mesh['fsdp'=4,'tp'=4,'sect'=2] {'sect'}, use_global_device_ids=true, to_apply=%region_1.0 | all-reduce | flops 1024 | bytes 8192 | tf_op jit(solution)/shard_map/psum | solution.py:33
  116.7 5.6 %psum.36 = f32[1024]{0:T(1024)S(1)} all-reduce(f32[1024]{0:T(1024)S(1)} %psum.35), channel_id=1, replica_groups=mesh['fsdp'=4,'tp'=4,'sect'=2] {'tp'}, use_global_device_ids=true, to_apply=%region_2.0 | all-reduce | flops 1024 | bytes 8192 | tf_op jit(solution)/shard_map/psum | solution.py:33
  122.3 0.2 convolution_bitcast_fusion.3
  122.5 0.2 fusion.3
  122.8 0.0 copy-done.2
  122.8 0.2 convert_reduce_fusion
  122.9 9.8 %all-reduce = (f32[2]{0:T(128)S(1)}, f32[2]{0:T(128)S(1)}) all-reduce(f32[2]{0:T(128)S(1)} %get-tuple-element.7, f32[2]{0:T(128)S(1)} %get-tuple-element.6), channel_id=1, replica_groups=mesh['fsdp'=4,'tp'=4,'sect'=2] {'fsdp'}, use_global_device_ids=true, to_apply=%region_4.5 | all-reduce | flops 4 | bytes 32 | tf_op jit(solution)/shard_map/psum | solution.py:51
  132.7 0.1 select_reduce_fusion.2
  132.8 0.1 select_reduce_fusion.1
  132.9 9.0 %psum.39 = f32[2]{0:T(128)S(1)} all-reduce(f32[2]{0:T(128)S(1)} %select_reduce_fusion.1), channel_id=1, replica_groups=mesh['fsdp'=4,'tp'=4,'sect'=2] {'fsdp'}, use_global_device_ids=true, to_apply=%region_9.10 | all-reduce | flops 2 | bytes 16 | tf_op jit(solution)/shard_map/psum | solution.py:55
  141.9 0.1 select_reduce_fusion
  142.0 1.0 copy.9
  143.0 0.5 rsqrt_multiply_fusion
  (6 shorter events, 0.0 us)
Async XLA Ops:
  7.2 104.0 %copy-start = (f32[256]{0:T(256)S(1)}, f32[256]{0:T(256)}, u32[]{:S(2)}) copy-start(f32[256]{0:T(256)} %param.8) | copy-start | bytes 3076
  7.2 50.9 %all-gather.5.cloned.1.call-start = ((), (), s32[]{:S(2)}) async-start(), calls=%async_computation.1 | async-start | bytes 2621440 | tf_op jit(solution)/shard_map/all_gather | solution.py:24
  9.5 95.2 %all-gather.3.cloned.1.call-start = ((), (), s32[]{:S(2)}) async-start(), calls=%async_computation | async-start | bytes 2621440 | tf_op jit(solution)/shard_map/all_gather | solution.py:27
  10.2 55.7 %copy-start.3 = (s32[1,4]{1,0:T(1,128)S(1)}, s32[1,4]{1,0:T(1,128)}, u32[]{:S(2)}) copy-start(s32[1,4]{1,0:T(1,128)} %param.9) | copy-start | bytes 52
  10.3 55.9 %copy-start.1 = (s32[1024]{0:T(1024)S(1)}, s32[1024]{0:T(1024)}, u32[]{:S(2)}) copy-start(s32[1024]{0:T(1024)} %param.10) | copy-start | bytes 12292
  64.4 40.3 %collective-permute-start = (f32[1024,256]{0,1:T(8,128)S(1)}, f32[1024,256]{0,1:T(8,128)S(1)}, u32[]{:S(2)}, u32[]{:S(2)}) collective-permute-start(f32[1024,256]{0,1:T(8,128)S(1)} %convolution_bitcast_fusion), channel_id=1, source_target_pairs={{0,1},{1,0},{2,3},{3,2},{4,5},{5,4},{6,7},{7,6},{8,9},{9,8},{10,11... | collective-permute-start | bytes 3145736 | tf_op jit(solution)/shard_map/ppermute | solution.py:11
  66.2 56.6 %copy-start.2 = (s32[4]{0:T(128)S(1)}, s32[4]{0:T(128)}, u32[]{:S(2)}) copy-start(s32[4]{0:T(128)} %param.11) | copy-start | bytes 52
Sparse Core Ops, SparseCore 0:
  9.6 48.3 all-gather.4
  60.2 44.4 all-gather.2
